TPU v7x, 512 devices: a whole 4x8x8 slice. The times are simulated.
512 devices in a mesh: dp: 64 (over z_lo, y, core), mp: 8 (over x, z_hi).
Axes of the slice: x: 4, y: 8, z: 8 (z_hi: 2, z_lo: 4; z = z_hi * 4 + z_lo), core: 2. Of those that a mesh axis runs over, the one named last changes fastest.
Arguments:
- activations: bfloat16 [65536, 4096], P('dp', 'mp'), may hold values from -6 to 6
- out_grad: bfloat16 [65536, 14336], P('dp', 'mp'), may hold values from -0.0234375 to 0.0234375
- tile_list: int32 [8, 64, 2], P('mp'), may hold values from 0 to 111, as said below
- tile_count: int32 [8], P('mp'), may hold values from 32 to 64, as said below
Outputs:
- grad_tiles: float32 [8, 64, 128, 128], P('mp', 'dp')
Inputs may be any that keep to these rules, and one draw needn't show every extreme that they name: `tile_list`: in shard c the 64 entries name distinct blocks; the block row lies in 0 to 31 and the block column in c * 14 to (c + 1) * 14 - 1. `tile_count`: some shard has all 64 slots live.
All inputs are finite; a program needn't handle non-finite values.
Results may differ from a plain program's by a relative error of at most 0.0003.
Values may be sent and summed in bfloat16 or wider, within the bound.
A program may use at most 128 MiB of HBM per device.

v0:
```python
import math
import jax
import jax.numpy as jnp
from jax import lax
from jax.sharding import PartitionSpec as P

D = 4096
BLK = 128


def on_device(activations, out_grad, tile_list, tile_count):
    gathered = lax.all_gather(activations, "mp", axis=1, tiled=True)
    token_count = gathered.shape[0]
    slot_total = tile_list.shape[1]
    col_blocks = out_grad.shape[1] // BLK
    row_ids = tile_list[0, :, 0]
    col_ids = tile_list[0, :, 1] - lax.axis_index("mp") * col_blocks
    active = (jnp.arange(slot_total, dtype=jnp.int32) < tile_count[0]).astype(jnp.float32)
    act_blocks = gathered.reshape(token_count, D // BLK, BLK)
    grad_blocks = out_grad.reshape(token_count, col_blocks, BLK)

    def group_product(indices):
        act_sel = jnp.take(act_blocks, indices[0], axis=1)
        grad_sel = jnp.take(grad_blocks, indices[1], axis=1)
        return jnp.einsum("tkr,tkc->krc", act_sel, grad_sel, preferred_element_type=jnp.float32)

    count = row_ids.shape[0]
    group_size = math.gcd(count, 16)
    result = lax.map(
        group_product, (row_ids.reshape(-1, group_size), col_ids.reshape(-1, group_size))
    )
    summed = lax.psum_scatter(
        result.reshape(count, BLK, BLK) * active[:, None, None],
        "dp",
        scatter_dimension=0,
        tiled=True,
    )
    return summed[None]


def solution(mesh):
    placed = (P("dp", "mp"), P("dp", "mp"), P("mp", None, None), P("mp"))
    return jax.shard_map(
        on_device, mesh=mesh, in_specs=placed, out_specs=P("mp", "dp", None, None), check_vma=False
    )
```

profile of v0, /device:TPU:2, one launch (start us, length us, event | category | flops | bytes accessed | tf_op | source)
XLA Modules:
  0.0 573.7 jit_solution(4600374275060258306)
XLA Ops:
  6.5 0.0 all-gather.2.cloned.1.call-start
  6.5 2.3 copy.11
  8.8 0.0 all-gather.2.cloned.1.call-update
  8.8 0.0 reduce-scatter.2.cloned.1.call-start
  8.9 0.8 subtract_reduce_fusion
  9.7 0.1 reshape_squeeze.3
  9.8 0.1 sub.12
  9.8 5.9 %copy.12 = bf16[1024,1792]{0,1:T(8,128)(2,1)} copy(bf16[1024,1792]{1,0:T(8,128)(2,1)} %param.7) | data formatting | bytes 7340032 | tf_op args[1]
  15.8 5.9 %copy.14 = bf16[1024,14,128]{2,0,1:T(8,128)(2,1)} copy(bf16[1024,14,128]{0,2,1:T(8,128)(2,1)} %bitcast.49) | data formatting | bytes 7340032 | tf_op jit(solution)/shard_map/while | solution.py:29
  22.3 171.0 %all-gather.2.cloned.1.call-done = bf16[1024,4096]{0,1:T(8,128)(2,1)} async-done(((bf16[1024,512]{0,1:T(8,128)(2,1)}), bf16[1024,4096]{0,1:T(8,128)(2,1)}) %all-gather.2.cloned.1.call-update) | async-done | bytes 8388624 | tf_op jit(solution)/shard_map/all_gather | solution.py:12
  193.3 11.9 %copy.13 = bf16[1024,32,128]{2,0,1:T(8,128)(2,1)} copy(bf16[1024,32,128]{0,2,1:T(8,128)(2,1)} %bitcast.50) | data formatting | bytes 16777216 | tf_op jit(solution)/shard_map/while | solution.py:29
  205.3 70.6 %while.10 = (s32[]{:T(128)}, f32[4,16,128,128]{3,2,1,0:T(8,128)}, s32[4,16]{1,0:T(4,128)S(1)}, bf16[1024,32,128]{2,0,1:T(8,128)(2,1)}, s32[4,16]{1,0:T(4,128)S(1)}, /*index=5*/bf16[1024,14,128]{2,0,1:T(8,128)(2,1)}, s32[]{:T(128)}) while((s32[]{:T(128)}, f32[4,16,128,128]{3,2,1,0:T(8,128)}, s32[4,16]{1,0:T(4,128)S(1)}, ...), condition=%wide.region_1.2_spmd, body=%wide.region_0.1_spmd.sunk | while | flops 541067584 | bytes 26223892 | solution.py:29
  205.3 5.1 gather_fusion
  210.4 6.4 %gather_fusion.1 = bf16[16,1024,128]{2,1,0:T(8,128)(2,1)} fusion(bf16[1024,32,128]{2,0,1:T(8,128)(2,1)} %get-tuple-element.130, s32[1024]{0:T(1024)S(1)} %pad_clamp_fusion.5), kind=kCustom, calls=%fused_computation.clone.1 | custom fusion | bytes 8388672 | tf_op jit(solution)/shard_map/while/body/eval_jaxpr/jit(_take)/gather | solution.py:23
  216.8 6.1 %fusion.28 = f32[4,16,128,128]{3,2,1,0:T(8,128)} fusion(f32[4,16,128,128]{3,2,1,0:T(8,128)} %get-tuple-element.121, s32[]{:T(128)} %get-tuple-element.120, bf16[16,1024,128]{2,1,0:T(8,128)(2,1)} %gather_fusion, pred[16]{0:T(512)(128)(4,1)S(1)} %get-tuple-element.110, bf16[16,1024,128]{2,1,0:T(8,128)(2,1)} %gather_fusion.1, ...), kind=kOutput, calls=%fused_computation.11.clone.1 | convolution fusion | flops 541065216 | bytes 9437728 | tf_op jit(solution)/shard_map/while/body/eval_jaxpr/tkr,tkc->krc/dot_general | solution.py:25
  222.9 5.1 gather_fusion
  228.0 6.4 %gather_fusion.1 = bf16[16,1024,128]{2,1,0:T(8,128)(2,1)} fusion(bf16[1024,32,128]{2,0,1:T(8,128)(2,1)} %get-tuple-element.130, s32[1024]{0:T(1024)S(1)} %pad_clamp_fusion.5), kind=kCustom, calls=%fused_computation.clone.1 | custom fusion | bytes 8388672 | tf_op jit(solution)/shard_map/while/body/eval_jaxpr/jit(_take)/gather | solution.py:23
  234.4 6.1 %fusion.28 = f32[4,16,128,128]{3,2,1,0:T(8,128)} fusion(f32[4,16,128,128]{3,2,1,0:T(8,128)} %get-tuple-element.121, s32[]{:T(128)} %get-tuple-element.120, bf16[16,1024,128]{2,1,0:T(8,128)(2,1)} %gather_fusion, pred[16]{0:T(512)(128)(4,1)S(1)} %get-tuple-element.110, bf16[16,1024,128]{2,1,0:T(8,128)(2,1)} %gather_fusion.1, ...), kind=kOutput, calls=%fused_computation.11.clone.1 | convolution fusion | flops 541065216 | bytes 9437728 | tf_op jit(solution)/shard_map/while/body/eval_jaxpr/tkr,tkc->krc/dot_general | solution.py:25
  240.6 5.1 gather_fusion
  245.7 6.4 %gather_fusion.1 = bf16[16,1024,128]{2,1,0:T(8,128)(2,1)} fusion(bf16[1024,32,128]{2,0,1:T(8,128)(2,1)} %get-tuple-element.130, s32[1024]{0:T(1024)S(1)} %pad_clamp_fusion.5), kind=kCustom, calls=%fused_computation.clone.1 | custom fusion | bytes 8388672 | tf_op jit(solution)/shard_map/while/body/eval_jaxpr/jit(_take)/gather | solution.py:23
  252.1 6.1 %fusion.28 = f32[4,16,128,128]{3,2,1,0:T(8,128)} fusion(f32[4,16,128,128]{3,2,1,0:T(8,128)} %get-tuple-element.121, s32[]{:T(128)} %get-tuple-element.120, bf16[16,1024,128]{2,1,0:T(8,128)(2,1)} %gather_fusion, pred[16]{0:T(512)(128)(4,1)S(1)} %get-tuple-element.110, bf16[16,1024,128]{2,1,0:T(8,128)(2,1)} %gather_fusion.1, ...), kind=kOutput, calls=%fused_computation.11.clone.1 | convolution fusion | flops 541065216 | bytes 9437728 | tf_op jit(solution)/shard_map/while/body/eval_jaxpr/tkr,tkc->krc/dot_general | solution.py:25
  258.2 5.1 gather_fusion
  263.3 6.4 %gather_fusion.1 = bf16[16,1024,128]{2,1,0:T(8,128)(2,1)} fusion(bf16[1024,32,128]{2,0,1:T(8,128)(2,1)} %get-tuple-element.130, s32[1024]{0:T(1024)S(1)} %pad_clamp_fusion.5), kind=kCustom, calls=%fused_computation.clone.1 | custom fusion | bytes 8388672 | tf_op jit(solution)/shard_map/while/body/eval_jaxpr/jit(_take)/gather | solution.py:23
  269.7 6.1 %fusion.28 = f32[4,16,128,128]{3,2,1,0:T(8,128)} fusion(f32[4,16,128,128]{3,2,1,0:T(8,128)} %get-tuple-element.121, s32[]{:T(128)} %get-tuple-element.120, bf16[16,1024,128]{2,1,0:T(8,128)(2,1)} %gather_fusion, pred[16]{0:T(512)(128)(4,1)S(1)} %get-tuple-element.110, bf16[16,1024,128]{2,1,0:T(8,128)(2,1)} %gather_fusion.1, ...), kind=kOutput, calls=%fused_computation.11.clone.1 | convolution fusion | flops 541065216 | bytes 9437728 | tf_op jit(solution)/shard_map/while/body/eval_jaxpr/tkr,tkc->krc/dot_general | solution.py:25
  275.8 4.5 bitcast_multiply_fusion
  280.3 0.0 reduce-scatter.2.cloned.1.call-update
  280.3 286.6 %reduce-scatter.2.cloned.1.call-done = f32[1,128,128]{2,1,0:T(8,128)} async-done(((f32[64,128,128]{2,1,0:T(8,128)}), f32[1,128,128]{2,1,0:T(8,128)}) %reduce-scatter.2.cloned.1.call-update) | async-done | bytes 65552 | tf_op jit(solution)/shard_map/reduce_scatter | solution.py:32
  (18 shorter events, 0.1 us)
Async XLA Ops:
  6.5 186.8 %all-gather.2.cloned.1.call-start = ((), (), s32[]{:S(2)}) async-start(), calls=%async_computation.1 | async-start | bytes 9437184 | tf_op jit(solution)/shard_map/all_gather | solution.py:12
  8.8 558.0 %reduce-scatter.2.cloned.1.call-start = ((), (), s32[]{:S(2)}) async-start(), calls=%async_computation.2 | async-start | bytes 4259840 | tf_op jit(solution)/shard_map/reduce_scatter | solution.py:32
Sparse Core Ops, SparseCore 0:
  10.5 182.7 all-gather.1
  280.4 286.3 reduce-scatter.1
where the time goes:
time: 575 us; the launch traced here: 574 us
  waiting for transfers between devices  458 us (80%)
  local copies, waits for them, and re-layouts  72.2 us (13%)
  matrix products  24.5 us (4%)
  between operations  14.1 us (2%)
    reduce_scatter x1, waiting for transfers between devices, on_device(): lax.psum_scatter(result.reshape(count, BLK, BLK) * active[:, None, None],...  287 us
    all_gather x1, waiting for transfers between devices, on_device(): gathered = lax.all_gather(activations, 'mp', axis=1, tiled=True)  171 us
    gather x4, local copies, waits for them, and re-layouts, group_product(): act_sel = jnp.take(act_blocks, indices[0], axis=1)  25.6 us
    dot_general x4, matrix products, group_product(): jnp.einsum('tkr,tkc->krc', act_sel, grad_sel, preferred_element_type=jnp....  24.5 us
    gather x4, local copies, waits for them, and re-layouts, group_product(): grad_sel = jnp.take(grad_blocks, indices[1], axis=1)  20.3 us
    while x2, local copies, waits for them, and re-layouts, on_device(): lax.map(group_product, (row_ids.reshape(-1, group_size), col_ids.reshape(...  17.8 us
  transfers between devices with their start and end apart: 2, of which 2 were waited for; matrix products, arithmetic and copies ran while one was open for 2% of the time, Pallas kernels for 0%

commit v1 on v0

--- a/solution.py
+++ b/solution.py
@@ -9,7 +9,9 @@
 
 
 def on_device(activations, out_grad, tile_list, tile_count):
-    gathered = lax.all_gather(activations, "mp", axis=1, tiled=True)
+    gathered = jnp.concatenate(
+        lax.all_to_all(jnp.stack([activations] * lax.axis_size("mp")), "mp", 0, 0), axis=1
+    )
     token_count = gathered.shape[0]
     slot_total = tile_list.shape[1]
     col_blocks = out_grad.shape[1] // BLK

time: 575 us -> 605 us (1.052)
  waiting for transfers between devices: 458 us -> 472 us
  starting transfers between devices: 0.04 us -> 13.4 us
    all_to_all x0 -> x1, waiting for transfers between devices: none -> 174 us  [on_device(): lax.all_to_all(jnp.stack([activations] * lax.axis_size('mp')), 'mp', 0, 0)]
    all_gather x1 -> x0, waiting for transfers between devices: 171 us -> none  [on_device(): gathered = lax.all_gather(activations, 'mp', axis=1, tiled=True)]
    all_to_all x0 -> x1, starting transfers between devices: none -> 13.4 us  [on_device(): lax.all_to_all(jnp.stack([activations] * lax.axis_size('mp')), 'mp', 0, 0)]
    reduce_scatter x1, waiting for transfers between devices: 287 us -> 297 us  [on_device(): lax.psum_scatter(result.reshape(count, BLK, BLK) * active[:, None, None],...]
where the time goes in v1:
time: 605 us; the launch traced here: 604 us
  waiting for transfers between devices  472 us (78%)
  local copies, waits for them, and re-layouts  75.6 us (12%)
  matrix products  24.5 us (4%)
  between operations  14.1 us (2%)
  starting transfers between devices  13.4 us (2%)
    reduce_scatter x1, waiting for transfers between devices, on_device(): lax.psum_scatter(result.reshape(count, BLK, BLK) * active[:, None, None],...  297 us
    all_to_all x1, waiting for transfers between devices, on_device(): lax.all_to_all(jnp.stack([activations] * lax.axis_size('mp')), 'mp', 0, 0)  174 us
    gather x4, local copies, waits for them, and re-layouts, group_product(): act_sel = jnp.take(act_blocks, indices[0], axis=1)  25.6 us
    dot_general x4, matrix products, group_product(): jnp.einsum('tkr,tkc->krc', act_sel, grad_sel, preferred_element_type=jnp....  24.5 us
    gather x4, local copies, waits for them, and re-layouts, group_product(): grad_sel = jnp.take(grad_blocks, indices[1], axis=1)  20.3 us
    while x2, local copies, waits for them, and re-layouts, on_device(): lax.map(group_product, (row_ids.reshape(-1, group_size), col_ids.reshape(...  17.8 us
    all_to_all x1, starting transfers between devices, on_device(): lax.all_to_all(jnp.stack([activations] * lax.axis_size('mp')), 'mp', 0, 0)  13.4 us
  transfers between devices with their start and end apart: 2, of which 2 were waited for; matrix products, arithmetic and copies ran while one was open for 2% of the time, Pallas kernels for 0%

profile of v1, /device:TPU:2, one launch (start us, length us, event | category | flops | bytes accessed | tf_op | source)
XLA Modules:
  0.0 603.8 jit_solution(13250337778743615635)
XLA Ops:
  6.5 1.5 copy.11
  8.0 4.3 stack.2
  12.3 0.0 copy-start
  12.3 13.4 %all-to-all-start = ((bf16[8,1024,512]{1,2,0:T(8,128)(2,1)}), bf16[8,1024,512]{1,2,0:T(8,128)(2,1)}, u32[]{:S(2)}, u32[]{:S(2)}) async-start(bf16[8,1024,512]{1,2,0:T(8,128)(2,1)} %stack.2), calls=%async_computation | async-start | bytes 16777216 | tf_op jit(solution)/shard_map/all_to_all | solution.py:13
  25.7 0.0 reduce-scatter.2.cloned.1.call-start
  25.7 0.0 copy-done
  25.8 0.1 reshape_squeeze.3
  25.8 0.1 sub.12
  25.9 5.9 copy.12
  31.8 5.9 copy.14
  38.4 174.1 %all-to-all-done = bf16[8,1024,512]{1,2,0:T(8,128)(2,1)} async-done(((bf16[8,1024,512]{1,2,0:T(8,128)(2,1)}), bf16[8,1024,512]{1,2,0:T(8,128)(2,1)}, u32[]{:S(2)}, u32[]{:S(2)}) %all-to-all-start) | async-done | bytes 8388640 | tf_op jit(solution)/shard_map/all_to_all | solution.py:13
  212.5 11.9 %copy.13 = bf16[1024,32,128]{2,0,1:T(8,128)(2,1)} copy(bf16[1024,32,128]{0,2,1:T(8,128)(2,1)} %bitcast.10) | data formatting | bytes 16777216 | tf_op jit(solution)/shard_map/while | solution.py:31
  224.4 70.6 %while.10 = (s32[]{:T(128)}, f32[4,16,128,128]{3,2,1,0:T(8,128)}, s32[4,16]{1,0:T(4,128)S(1)}, bf16[1024,32,128]{2,0,1:T(8,128)(2,1)}, s32[4,16]{1,0:T(4,128)S(1)}, /*index=5*/bf16[1024,14,128]{2,0,1:T(8,128)(2,1)}, s32[]{:T(128)}) while((s32[]{:T(128)}, f32[4,16,128,128]{3,2,1,0:T(8,128)}, s32[4,16]{1,0:T(4,128)S(1)}, ...), condition=%wide.region_1.2_spmd, body=%wide.region_0.1_spmd.sunk | while | flops 541067584 | bytes 26223892 | solution.py:31
  224.5 5.1 gather_fusion
  229.5 6.4 %gather_fusion.1 = bf16[16,1024,128]{2,1,0:T(8,128)(2,1)} fusion(bf16[1024,32,128]{2,0,1:T(8,128)(2,1)} %get-tuple-element.130, s32[1024]{0:T(1024)S(1)} %pad_clamp_fusion.5), kind=kCustom, calls=%fused_computation.clone.1 | custom fusion | bytes 8388672 | tf_op jit(solution)/shard_map/while/body/eval_jaxpr/jit(_take)/gather | solution.py:25
  236.0 6.1 %fusion.28 = f32[4,16,128,128]{3,2,1,0:T(8,128)} fusion(f32[4,16,128,128]{3,2,1,0:T(8,128)} %get-tuple-element.121, s32[]{:T(128)} %get-tuple-element.120, bf16[16,1024,128]{2,1,0:T(8,128)(2,1)} %gather_fusion, pred[16]{0:T(512)(128)(4,1)S(1)} %get-tuple-element.110, bf16[16,1024,128]{2,1,0:T(8,128)(2,1)} %gather_fusion.1, ...), kind=kOutput, calls=%fused_computation.11.clone.1 | convolution fusion | flops 541065216 | bytes 9437728 | tf_op jit(solution)/shard_map/while/body/eval_jaxpr/tkr,tkc->krc/dot_general | solution.py:27
  242.1 5.1 gather_fusion
  247.2 6.4 %gather_fusion.1 = bf16[16,1024,128]{2,1,0:T(8,128)(2,1)} fusion(bf16[1024,32,128]{2,0,1:T(8,128)(2,1)} %get-tuple-element.130, s32[1024]{0:T(1024)S(1)} %pad_clamp_fusion.5), kind=kCustom, calls=%fused_computation.clone.1 | custom fusion | bytes 8388672 | tf_op jit(solution)/shard_map/while/body/eval_jaxpr/jit(_take)/gather | solution.py:25
  253.6 6.1 %fusion.28 = f32[4,16,128,128]{3,2,1,0:T(8,128)} fusion(f32[4,16,128,128]{3,2,1,0:T(8,128)} %get-tuple-element.121, s32[]{:T(128)} %get-tuple-element.120, bf16[16,1024,128]{2,1,0:T(8,128)(2,1)} %gather_fusion, pred[16]{0:T(512)(128)(4,1)S(1)} %get-tuple-element.110, bf16[16,1024,128]{2,1,0:T(8,128)(2,1)} %gather_fusion.1, ...), kind=kOutput, calls=%fused_computation.11.clone.1 | convolution fusion | flops 541065216 | bytes 9437728 | tf_op jit(solution)/shard_map/while/body/eval_jaxpr/tkr,tkc->krc/dot_general | solution.py:27
  259.8 5.1 gather_fusion
  264.8 6.4 %gather_fusion.1 = bf16[16,1024,128]{2,1,0:T(8,128)(2,1)} fusion(bf16[1024,32,128]{2,0,1:T(8,128)(2,1)} %get-tuple-element.130, s32[1024]{0:T(1024)S(1)} %pad_clamp_fusion.5), kind=kCustom, calls=%fused_computation.clone.1 | custom fusion | bytes 8388672 | tf_op jit(solution)/shard_map/while/body/eval_jaxpr/jit(_take)/gather | solution.py:25
  271.3 6.1 %fusion.28 = f32[4,16,128,128]{3,2,1,0:T(8,128)} fusion(f32[4,16,128,128]{3,2,1,0:T(8,128)} %get-tuple-element.121, s32[]{:T(128)} %get-tuple-element.120, bf16[16,1024,128]{2,1,0:T(8,128)(2,1)} %gather_fusion, pred[16]{0:T(512)(128)(4,1)S(1)} %get-tuple-element.110, bf16[16,1024,128]{2,1,0:T(8,128)(2,1)} %gather_fusion.1, ...), kind=kOutput, calls=%fused_computation.11.clone.1 | convolution fusion | flops 541065216 | bytes 9437728 | tf_op jit(solution)/shard_map/while/body/eval_jaxpr/tkr,tkc->krc/dot_general | solution.py:27
  277.4 5.1 gather_fusion
  282.5 6.4 %gather_fusion.1 = bf16[16,1024,128]{2,1,0:T(8,128)(2,1)} fusion(bf16[1024,32,128]{2,0,1:T(8,128)(2,1)} %get-tuple-element.130, s32[1024]{0:T(1024)S(1)} %pad_clamp_fusion.5), kind=kCustom, calls=%fused_computation.clone.1 | custom fusion | bytes 8388672 | tf_op jit(solution)/shard_map/while/body/eval_jaxpr/jit(_take)/gather | solution.py:25
  288.9 6.1 %fusion.28 = f32[4,16,128,128]{3,2,1,0:T(8,128)} fusion(f32[4,16,128,128]{3,2,1,0:T(8,128)} %get-tuple-element.121, s32[]{:T(128)} %get-tuple-element.120, bf16[16,1024,128]{2,1,0:T(8,128)(2,1)} %gather_fusion, pred[16]{0:T(512)(128)(4,1)S(1)} %get-tuple-element.110, bf16[16,1024,128]{2,1,0:T(8,128)(2,1)} %gather_fusion.1, ...), kind=kOutput, calls=%fused_computation.11.clone.1 | convolution fusion | flops 541065216 | bytes 9437728 | tf_op jit(solution)/shard_map/while/body/eval_jaxpr/tkr,tkc->krc/dot_general | solution.py:27
  295.0 4.5 bitcast_multiply_fusion
  299.5 0.0 reduce-scatter.2.cloned.1.call-update
  299.5 297.5 %reduce-scatter.2.cloned.1.call-done = f32[1,128,128]{2,1,0:T(8,128)} async-done(((f32[64,128,128]{2,1,0:T(8,128)}), f32[1,128,128]{2,1,0:T(8,128)}) %reduce-scatter.2.cloned.1.call-update) | async-done | bytes 65552 | tf_op jit(solution)/shard_map/reduce_scatter | solution.py:34
  (19 shorter events, 0.1 us)
Async XLA Ops:
  12.3 13.4 %copy-start = (s32[1,64,2]{1,2,0:T(2,128)S(1)}, s32[1,64,2]{1,2,0:T(2,128)}, u32[]{:S(2)}) copy-start(s32[1,64,2]{1,2,0:T(2,128)} %param.8) | copy-start | bytes 1540
  12.3 200.2 %all-to-all-start = ((bf16[8,1024,512]{1,2,0:T(8,128)(2,1)}), bf16[8,1024,512]{1,2,0:T(8,128)(2,1)}, u32[]{:S(2)}, u32[]{:S(2)}) async-start(bf16[8,1024,512]{1,2,0:T(8,128)(2,1)} %stack.2), calls=%async_computation | async-start | bytes 16777216 | tf_op jit(solution)/shard_map/all_to_all | solution.py:13
  25.7 571.2 %reduce-scatter.2.cloned.1.call-start = ((), (), s32[]{:S(2)}) async-start(), calls=%async_computation.2 | async-start | bytes 4259840 | tf_op jit(solution)/shard_map/reduce_scatter | solution.py:34
Sparse Core Ops, SparseCore 0:
  299.6 297.2 reduce-scatter.1
